TPU v7x, 128 devices: a whole 4x4x4 slice. The times are simulated.
128 devices in a mesh: leaf: 4 (over y), rows: 32 (over z, x, core).
Axes of the slice: x: 4, y: 4, z: 4, core: 2. Of those that a mesh axis runs over, the one named last changes fastest.
Arguments:
- leaf_rhs: float32 [8, 16, 2048], P(None, 'leaf', 'rows'), may hold values from -6 to 6
- parent_rhs: float32 [8, 4, 4096], P(None, 'leaf', 'rows'), may hold values from -6 to 6
- root_rhs: float32 [8, 4096], P(None, ('leaf', 'rows')), may hold values from -6 to 6
- leaf_inv: bfloat16 [16, 2048, 2048], P('leaf', 'rows'), as said below
- leaf_panel: bfloat16 [16, 8192, 2048], P('leaf', 'rows'), may hold values from -0.0625 to 0.0625
- leaf_rows: int32 [16, 8192], P('leaf', 'rows'), may hold values from 0 to 8191, as said below
- leaf_height: int32 [16], P('leaf'), may hold values from 2048 to 8192
- parent_inv: bfloat16 [4, 4096, 4096], P('leaf', 'rows'), as said below
- parent_panel: bfloat16 [4, 4096, 4096], P('leaf', 'rows'), may hold values from -0.046875 to 0.046875
- parent_rows: int32 [4, 4096], P('leaf', 'rows'), may hold values from 0 to 4095, as said below
- parent_height: int32 [4], P('leaf'), may hold values from 1024 to 4096
- root_inv: bfloat16 [4096, 4096], P('rows'), as said below
Outputs:
- leaf_solution: float32 [8, 16, 2048], P(None, 'leaf', 'rows')
- parent_solution: float32 [8, 4, 4096], P(None, 'leaf', 'rows')
- root_solution: float32 [8, 4096], P(None, ('leaf', 'rows'))
Inputs may be any that keep to these rules, and one draw needn't show every extreme that they name: `leaf_rows`: each leaf's first leaf_height entries are distinct and ascending; every entry is a valid ancestor index. `parent_rows`: each parent's first parent_height entries are distinct and ascending. `leaf_inv`: A dense well conditioned matrix. `parent_inv`: A dense well conditioned matrix. `root_inv`: A dense well conditioned matrix.
All inputs are finite; a program needn't handle non-finite values.
Results may differ from a plain program's by a relative error of at most 0.009.
Values may be sent and summed in bfloat16 or wider, within the bound.
A program may use at most 64 MiB of HBM per device.

v0:
```python
import jax
import jax.numpy as jnp
from jax import lax
from jax.sharding import PartitionSpec as P


def shards(
    leaf_rhs,
    parent_rhs,
    root_rhs,
    leaf_inv,
    leaf_panel,
    leaf_rows,
    leaf_height,
    parent_inv,
    parent_panel,
    parent_rows,
    parent_height,
    root_inv,
):
    rcount = leaf_rhs.shape[0]
    group_leaves = leaf_rhs.shape[1]
    leaf_local = leaf_panel.shape[1]
    parent_width = parent_inv.shape[2]
    root_width = root_inv.shape[1]
    row_index = lax.axis_index("rows")
    parent_cols = parent_rhs.shape[2]
    root_cols = root_rhs.shape[1]
    flat_index = lax.axis_index("leaf") * lax.axis_size("rows") + row_index
    block = leaf_inv
    ly = jnp.einsum(
        "rln,lin->rli",
        lax.all_gather(leaf_rhs.astype(jnp.bfloat16), "rows", axis=2, tiled=True),
        block,
        preferred_element_type=jnp.float32,
    )
    lyb = ly.astype(jnp.bfloat16)
    block = leaf_panel
    lupd = jnp.einsum(
        "rln,lhn->rlh",
        lax.all_gather(lyb, "rows", axis=2, tiled=True),
        block,
        preferred_element_type=jnp.float32,
    )
    leaf_pos = row_index * leaf_local + jnp.arange(leaf_local, dtype=jnp.int32)
    leaf_mask = leaf_pos[None, :] < leaf_height[:, None]
    lupd = jnp.where(leaf_mask[None, :, :], lupd, 0.0)
    leaf_flat = leaf_rows.reshape(-1)
    local_acc = (
        jnp.zeros((rcount, parent_width + root_width), jnp.float32)
        .at[:, leaf_flat]
        .add(lupd.reshape(rcount, -1))
    )
    group_acc = lax.psum(local_acc, "rows")
    parent_acc = group_acc[:, :parent_width]
    root_from_leaves = lax.psum(group_acc[:, parent_width:], "leaf")
    parent_slice = lax.dynamic_slice_in_dim(parent_acc, row_index * parent_cols, parent_cols, 1)
    prb = (parent_rhs[:, 0, :] - parent_slice).astype(jnp.bfloat16)
    inverse_rows = parent_inv[0]
    panel_rows = parent_panel[0]
    block = inverse_rows
    py = jnp.dot(
        lax.all_gather(prb, "rows", axis=1, tiled=True), block.T, preferred_element_type=jnp.float32
    )
    pyb = py.astype(jnp.bfloat16)
    parent_local = panel_rows.shape[0]
    block = panel_rows
    pupd = jnp.dot(
        lax.all_gather(pyb, "rows", axis=1, tiled=True), block.T, preferred_element_type=jnp.float32
    )
    parent_pos = row_index * parent_local + jnp.arange(parent_local, dtype=jnp.int32)
    parent_mask = parent_pos < parent_height[0]
    pupd = jnp.where(parent_mask[None, :], pupd, 0.0)
    parent_root = jnp.zeros((rcount, root_width), jnp.float32).at[:, parent_rows[0]].add(pupd)
    root_acc = root_from_leaves + lax.psum(parent_root, ("leaf", "rows"))
    root_slice = lax.dynamic_slice_in_dim(root_acc, flat_index * root_cols, root_cols, 1)
    rrb = (root_rhs - root_slice).astype(jnp.bfloat16)
    block = root_inv
    ry = jnp.dot(
        lax.all_gather(rrb, ("leaf", "rows"), axis=1, tiled=True),
        block.T,
        preferred_element_type=jnp.float32,
    )
    root_term = jnp.dot(ry.astype(jnp.bfloat16), root_inv, preferred_element_type=jnp.float32)
    root_full = lax.psum(root_term, "rows")
    root_solution = lax.dynamic_slice_in_dim(root_full, flat_index * root_cols, root_cols, 1)
    rxb = root_full.astype(jnp.bfloat16)
    parent_anc = rxb[:, parent_rows[0]]
    parent_anc = jnp.where(parent_mask[None, :], parent_anc, jnp.zeros_like(parent_anc))
    parent_term = jnp.dot(parent_anc, panel_rows, preferred_element_type=jnp.float32)
    parent_tail = lax.psum_scatter(parent_term, "rows", scatter_dimension=1, tiled=True)
    pvb = (py - parent_tail).astype(jnp.bfloat16)
    parent_sol_term = jnp.dot(pvb, inverse_rows, preferred_element_type=jnp.float32)
    parent_sol = lax.psum_scatter(parent_sol_term, "rows", scatter_dimension=1, tiled=True)
    parent_whole = lax.all_gather(parent_sol.astype(jnp.bfloat16), "rows", axis=1, tiled=True)
    ancestors = jnp.concatenate([parent_whole, rxb], axis=1)
    leaf_anc = ancestors[:, leaf_flat].reshape(rcount, group_leaves, leaf_local)
    leaf_anc = jnp.where(leaf_mask[None, :, :], leaf_anc, jnp.zeros_like(leaf_anc))
    leaf_term = jnp.einsum("rlh,lhc->rlc", leaf_anc, leaf_panel, preferred_element_type=jnp.float32)
    leaf_tail = lax.psum_scatter(leaf_term, "rows", scatter_dimension=2, tiled=True)
    lvb = (ly - leaf_tail).astype(jnp.bfloat16)
    leaf_sol_term = jnp.einsum("rli,lic->rlc", lvb, leaf_inv, preferred_element_type=jnp.float32)
    leaf_sol = lax.psum_scatter(leaf_sol_term, "rows", scatter_dimension=2, tiled=True)
    return (leaf_sol, parent_sol[:, None, :], root_solution)


def solution(mesh):
    return jax.shard_map(
        shards,
        mesh=mesh,
        in_specs=(
            P(None, "leaf", "rows"),
            P(None, "leaf", "rows"),
            P(None, ("leaf", "rows")),
            P("leaf", "rows", None),
            P("leaf", "rows", None),
            P("leaf", "rows"),
            P("leaf"),
            P("leaf", "rows", None),
            P("leaf", "rows", None),
            P("leaf", "rows"),
            P("leaf"),
            P("rows", None),
        ),
        out_specs=(P(None, "leaf", "rows"), P(None, "leaf", "rows"), P(None, ("leaf", "rows"))),
        check_vma=False,
    )
```

profile of v0, /device:TPU:0, one launch (start us, length us, event | category | flops | bytes accessed | tf_op | source)
XLA Modules:
  0.0 916.0 jit_solution(10626270217796478974)
XLA Ops:
  8.9 27.5 %all_gather.18 = bf16[8,4,2048]{0,1,2:T(4,128)(2,1)S(1)} all-gather(bf16[8,4,64]{0,1,2:T(4,128)(2,1)S(1)} %copy.62), channel_id=1, replica_groups=mesh['leaf'=4,'rows'=32] {'rows'}, dimensions={2}, use_global_device_ids=true | all-gather | bytes 135168 | tf_op jit(solution)/shard_map/all_gather | solution.py:33
  37.3 25.3 %all_gather.19 = bf16[8,4,2048]{0,1,2:T(4,128)(2,1)S(1)} all-gather(bf16[8,4,64]{0,1,2:T(4,128)(2,1)S(1)} %copy.64), channel_id=1, replica_groups=mesh['leaf'=4,'rows'=32] {'rows'}, dimensions={2}, use_global_device_ids=true | all-gather | bytes 135168 | tf_op jit(solution)/shard_map/all_gather | solution.py:41
  62.7 3.4 fusion.6
  66.3 8.2 scatter_custom_fusion
  74.5 3.5 copy.67
  78.9 100.7 %all-reduce.5.cloned.1.call-done = f32[8,8192]{1,0:T(8,128)} async-done(((f32[8,8192]{1,0:T(8,128)}), f32[8,8192]{1,0:T(8,128)}) %all-reduce.5.cloned.1.call-update) | async-done | bytes 262160 | tf_op jit(solution)/shard_map/psum | solution.py:54
  181.2 24.6 %all_gather.20 = bf16[8,4096]{1,0:T(8,128)(2,1)S(1)} all-gather(bf16[8,128]{1,0:T(8,128)(2,1)S(1)} %subtract_convert_fusion.3), channel_id=1, replica_groups=mesh['leaf'=4,'rows'=32] {'rows'}, dimensions={1}, use_global_device_ids=true | all-gather | bytes 67584 | tf_op jit(solution)/shard_map/all_gather | solution.py:63
  206.2 21.5 %all_gather.21 = bf16[8,4096]{1,0:T(8,128)(2,1)S(1)} all-gather(bf16[8,128]{1,0:T(8,128)(2,1)S(1)} %get-tuple-element.22), channel_id=1, replica_groups=mesh['leaf'=4,'rows'=32] {'rows'}, dimensions={1}, use_global_device_ids=true | all-gather | bytes 67584 | tf_op jit(solution)/shard_map/all_gather | solution.py:69
  231.8 141.0 %all-reduce.9.cloned.1.call-done = f32[8,4096]{1,0:T(8,128)} async-done(((f32[8,4096]{1,0:T(8,128)}), f32[8,4096]{1,0:T(8,128)}) %all-reduce.9.cloned.1.call-update) | async-done | bytes 131088 | tf_op jit(solution)/shard_map/psum | solution.py:75
  372.8 41.1 %all-reduce.7.cloned.1.call-done = f32[8,4096]{1,0:T(8,128)} async-done(((f32[8,4096]{1,0:T(8,128)}), f32[8,4096]{1,0:T(8,128)}) %all-reduce.7.cloned.1.call-update) | async-done | bytes 131088 | tf_op jit(solution)/shard_map/psum | solution.py:56
  414.7 35.9 %all-gather = bf16[128,32,8]{1,2,0:T(8,128)(2,1)S(1)} all-gather(bf16[1,32,8]{1,2,0:T(8,128)(2,1)S(1)} %fusion.31), channel_id=1, replica_groups=mesh['leaf'=4,'rows'=32] {'leaf','rows'}, dimensions={0}, use_global_device_ids=true | all-gather | bytes 66048 | tf_op jit(solution)/shard_map/all_gather | solution.py:80
  450.9 3.2 fusion.13
  454.2 98.7 %all-reduce.11.cloned.1.call-done = f32[8,4096]{1,0:T(8,128)} async-done(((f32[8,4096]{1,0:T(8,128)}), f32[8,4096]{1,0:T(8,128)}) %all-reduce.11.cloned.1.call-update) | async-done | bytes 131088 | tf_op jit(solution)/shard_map/psum | solution.py:85
  558.2 71.9 %reduce-scatter.9.cloned.1.call-done = f32[8,128]{1,0:T(8,128)} async-done(((f32[8,4096]{1,0:T(8,128)}), f32[8,128]{1,0:T(8,128)}) %reduce-scatter.9.cloned.1.call-update) | async-done | bytes 4112 | tf_op jit(solution)/shard_map/reduce_scatter | solution.py:91
  631.7 73.8 %reduce-scatter.11.cloned.1.call-done = f32[8,128]{1,0:T(8,128)} async-done(((f32[8,4096]{1,0:T(8,128)}), f32[8,128]{1,0:T(8,128)}) %reduce-scatter.11.cloned.1.call-update) | async-done | bytes 4112 | tf_op jit(solution)/shard_map/reduce_scatter | solution.py:94
  706.2 23.5 %all_gather.23 = bf16[8,4096]{1,0:T(8,128)(2,1)S(1)} all-gather(bf16[8,128]{1,0:T(8,128)(2,1)S(1)} %convert_element_type.38), channel_id=1, replica_groups=mesh['leaf'=4,'rows'=32] {'rows'}, dimensions={1}, use_global_device_ids=true | all-gather | bytes 67584 | tf_op jit(solution)/shard_map/all_gather | solution.py:95
  730.7 3.2 gather_fusion.1
  734.1 2.8 convolution_bitcast_fusion.1
  736.9 3.1 copy.76
  740.0 4.5 reshape.143
  744.6 76.7 %reduce-scatter.13.cloned.1.call-done = f32[64,32]{1,0:T(8,128)} async-done(((f32[2048,32]{1,0:T(8,128)}), f32[64,32]{1,0:T(8,128)}) %reduce-scatter.13.cloned.1.call-update) | async-done | bytes 8208
  822.6 3.1 copy.78
  825.6 4.5 reshape.145
  831.6 76.0 %reduce-scatter.15.cloned.1.call-done = f32[64,32]{1,0:T(8,128)} async-done(((f32[2048,32]{1,0:T(8,128)}), f32[64,32]{1,0:T(8,128)}) %reduce-scatter.15.cloned.1.call-update) | async-done | bytes 8208
  (72 shorter events, 23.1 us)
Async XLA Ops:
  7.2 29.2 %copy-start = (bf16[4,64,2048]{2,1,0:T(8,128)(2,1)S(1)}, bf16[4,64,2048]{2,1,0:T(8,128)(2,1)}, u32[]{:S(2)}) copy-start(bf16[4,64,2048]{2,1,0:T(8,128)(2,1)} %param.15) | copy-start | bytes 3145732
  7.2 172.4 %all-reduce.5.cloned.1.call-start = ((), (), s32[]{:S(2)}) async-start(), calls=%async_computation.4 | async-start | bytes 524288 | tf_op jit(solution)/shard_map/psum | solution.py:54
  36.3 26.3 %copy-start.7 = (s32[4]{0:T(128)S(1)}, s32[4]{0:T(128)}, u32[]{:S(2)}) copy-start(s32[4]{0:T(128)} %param.18) | copy-start | bytes 52
  74.5 3.6 copy-start.8
  74.5 106.7 %copy-start.5 = (f32[8,1,128]{2,1,0:T(1,128)S(1)}, f32[8,1,128]{2,1,0:T(1,128)}, u32[]{:S(2)}) copy-start(f32[8,1,128]{2,1,0:T(1,128)} %param.13) | copy-start | bytes 12292
  74.5 131.4 %copy-start.3 = (bf16[1,128,4096]{2,1,0:T(8,128)(2,1)S(1)}, bf16[1,128,4096]{2,1,0:T(8,128)(2,1)}, u32[]{:S(2)}) copy-start(bf16[1,128,4096]{2,1,0:T(8,128)(2,1)} %param.19) | copy-start | bytes 3145732
  78.0 149.7 %copy-start.1 = (bf16[1,128,4096]{2,1,0:T(8,128)(2,1)S(1)}, bf16[1,128,4096]{2,1,0:T(8,128)(2,1)}, u32[]{:S(2)}) copy-start(bf16[1,128,4096]{2,1,0:T(8,128)(2,1)} %param.20) | copy-start | bytes 3145732
  78.1 294.8 %all-reduce.9.cloned.1.call-start = ((), (), s32[]{:S(2)}) async-start(), calls=%async_computation.6 | async-start | bytes 262144 | tf_op jit(solution)/shard_map/psum | solution.py:75
  228.2 185.7 %copy-start.6 = (f32[8,32]{1,0:T(8,128)S(1)}, f32[8,32]{1,0:T(8,128)}, u32[]{:S(2)}) copy-start(f32[8,32]{1,0:T(8,128)} %param.14) | copy-start | bytes 3076
  231.0 182.9 %all-reduce.7.cloned.1.call-start = ((), (), s32[]{:S(2)}) async-start(), calls=%async_computation.5 | async-start | bytes 262144 | tf_op jit(solution)/shard_map/psum | solution.py:56
  231.8 321.1 %all-reduce.11.cloned.1.call-start = ((), (), s32[]{:S(2)}) async-start(), calls=%async_computation.7 | async-start | bytes 262144 | tf_op jit(solution)/shard_map/psum | solution.py:85
  450.6 106.5 %copy-start.2 = (bf16[1,128,4096]{2,1,0:T(8,128)(2,1)S(1)}, bf16[1,128,4096]{2,1,0:T(8,128)(2,1)}, u32[]{:S(2)}) copy-start(bf16[1,128,4096]{2,1,0:T(8,128)(2,1)} %param.20) | copy-start | bytes 3145732
  450.9 179.2 %copy-start.4 = (bf16[1,128,4096]{2,1,0:T(8,128)(2,1)S(1)}, bf16[1,128,4096]{2,1,0:T(8,128)(2,1)}, u32[]{:S(2)}) copy-start(bf16[1,128,4096]{2,1,0:T(8,128)(2,1)} %param.19) | copy-start | bytes 3145732
  454.1 176.0 %reduce-scatter.9.cloned.1.call-start = ((), (), s32[]{:S(2)}) async-start(), calls=%async_computation.8 | async-start | bytes 135168 | tf_op jit(solution)/shard_map/reduce_scatter | solution.py:91
  558.1 147.3 %reduce-scatter.11.cloned.1.call-start = ((), (), s32[]{:S(2)}) async-start(), calls=%async_computation.9 | async-start | bytes 135168 | tf_op jit(solution)/shard_map/reduce_scatter | solution.py:94
  631.7 189.7 %reduce-scatter.13.cloned.1.call-start = ((), (), s32[]{:S(2)}) async-start(), calls=%async_computation.10 | async-start | bytes 1081344
  744.6 163.0 %reduce-scatter.15.cloned.1.call-start = ((), (), s32[]{:S(2)}) async-start(), calls=%async_computation.11 | async-start | bytes 1081344
Sparse Core Ops, SparseCore 0:
  78.2 101.3 all-reduce.4
  231.2 141.6 all-reduce.8
  375.1 38.7 all-reduce.6
  454.2 98.5 all-reduce.10
  558.3 71.7 reduce-scatter.8
  633.9 71.5 reduce-scatter.10
  744.7 76.6 reduce-scatter.12
  830.3 77.2 reduce-scatter.14
where the time goes:
time: 917 us; the launch traced here: 916 us
  waiting for transfers between devices  681 us (74%)
  blocking collectives  158 us (17%)
  local copies, waits for them, and re-layouts  35.6 us (4%)
  between operations  15 us (2%)
  matrix products  13.8 us (2%)
  other arithmetic  12.2 us (1%)
    unnamed x10, waiting for transfers between devices  154 us
    psum x1, waiting for transfers between devices, shards(): root_acc = root_from_leaves + lax.psum(parent_root, ('leaf', 'rows'))  141 us
    psum x1, waiting for transfers between devices, shards(): group_acc = lax.psum(local_acc, 'rows')  101 us
    psum x1, waiting for transfers between devices, shards(): root_full = lax.psum(root_term, 'rows')  98.7 us
    reduce_scatter x1, waiting for transfers between devices, shards(): lax.psum_scatter(parent_sol_term, 'rows', scatter_dimension=1, tiled=True)  73.8 us
    reduce_scatter x1, waiting for transfers between devices, shards(): lax.psum_scatter(parent_term, 'rows', scatter_dimension=1, tiled=True)  71.9 us
    psum x1, waiting for transfers between devices, shards(): root_from_leaves = lax.psum(group_acc[:, parent_width:], 'leaf')  41.1 us
    all_gather x1, blocking collectives, shards(): lax.all_gather(rrb, ('leaf', 'rows'), axis=1, tiled=True)  35.9 us
  transfers between devices with their start and end apart: 8, of which 8 were waited for; matrix products, arithmetic and copies ran while one was open for 0% of the time, Pallas kernels for 0%

commit v1 on v0

--- a/solution.py
+++ b/solution.py
@@ -82,7 +82,11 @@
         preferred_element_type=jnp.float32,
     )
     root_term = jnp.dot(ry.astype(jnp.bfloat16), root_inv, preferred_element_type=jnp.float32)
-    root_full = lax.psum(root_term, "rows")
+    root_full = root_term
+    for hop in (1, 2, 4, 8, 16):
+        root_full = root_full + lax.ppermute(
+            root_full, "rows", [(dev, dev ^ hop) for dev in range(32)]
+        )
     root_solution = lax.dynamic_slice_in_dim(root_full, flat_index * root_cols, root_cols, 1)
     rxb = root_full.astype(jnp.bfloat16)
     parent_anc = rxb[:, parent_rows[0]]

time: 917 us -> 841 us (0.917)
  waiting for transfers between devices: 681 us -> 601 us
    psum x1 -> x0, waiting for transfers between devices: 98.7 us -> none  [shards(): root_full = lax.psum(root_term, 'rows')]
    ppermute x0 -> x5, waiting for transfers between devices: none -> 20.4 us  [shards(): lax.ppermute(root_full, 'rows', [(dev, dev ^ hop) for dev in range(32)])]
    unnamed x10 -> x9, waiting for transfers between devices: 154 us -> 154 us
    unnamed x29 -> x31, local copies, waits for them, and re-layouts: 19.6 us -> 19.5 us
  transfers between devices with their start and end apart: 8 -> 12, of which waited for: 8 -> 12; matrix products, arithmetic and copies ran while one was open for 0% -> 0% of each run, Pallas kernels for 0% -> 0%
where the time goes in v1:
time: 841 us; the launch traced here: 840 us
  waiting for transfers between devices  601 us (71%)
  blocking collectives  158 us (19%)
  local copies, waits for them, and re-layouts  35.3 us (4%)
  between operations  15 us (2%)
  matrix products  13.1 us (2%)
  other arithmetic  11.9 us (1%)
    unnamed x9, waiting for transfers between devices  154 us
    psum x1, waiting for transfers between devices, shards(): root_acc = root_from_leaves + lax.psum(parent_root, ('leaf', 'rows'))  141 us
    psum x1, waiting for transfers between devices, shards(): group_acc = lax.psum(local_acc, 'rows')  101 us
    reduce_scatter x1, waiting for transfers between devices, shards(): lax.psum_scatter(parent_sol_term, 'rows', scatter_dimension=1, tiled=True)  73.1 us
    reduce_scatter x1, waiting for transfers between devices, shards(): lax.psum_scatter(parent_term, 'rows', scatter_dimension=1, tiled=True)  70.2 us
    psum x1, waiting for transfers between devices, shards(): root_from_leaves = lax.psum(group_acc[:, parent_width:], 'leaf')  41.1 us
    all_gather x1, blocking collectives, shards(): lax.all_gather(rrb, ('leaf', 'rows'), axis=1, tiled=True)  35.9 us
    all_gather x1, blocking collectives, shards(): lax.all_gather(leaf_rhs.astype(jnp.bfloat16), 'rows', axis=2, tiled=True)  27.5 us
  transfers between devices with their start and end apart: 12, of which 12 were waited for; matrix products, arithmetic and copies ran while one was open for 0% of the time, Pallas kernels for 0%

profile of v1, /device:TPU:0, one launch (start us, length us, event | category | flops | bytes accessed | tf_op | source)
XLA Modules:
  0.0 839.8 jit_solution(9282782583743233189)
XLA Ops:
  8.9 27.5 %all_gather.18 = bf16[8,4,2048]{0,1,2:T(4,128)(2,1)S(1)} all-gather(bf16[8,4,64]{0,1,2:T(4,128)(2,1)S(1)} %copy.62), channel_id=1, replica_groups=mesh['leaf'=4,'rows'=32] {'rows'}, dimensions={2}, use_global_device_ids=true | all-gather | bytes 135168 | tf_op jit(solution)/shard_map/all_gather | solution.py:33
  37.3 25.3 %all_gather.19 = bf16[8,4,2048]{0,1,2:T(4,128)(2,1)S(1)} all-gather(bf16[8,4,64]{0,1,2:T(4,128)(2,1)S(1)} %copy.64), channel_id=1, replica_groups=mesh['leaf'=4,'rows'=32] {'rows'}, dimensions={2}, use_global_device_ids=true | all-gather | bytes 135168 | tf_op jit(solution)/shard_map/all_gather | solution.py:41
  62.7 3.4 fusion.6
  66.3 8.2 scatter_custom_fusion
  74.5 3.5 copy.67
  78.9 100.7 %all-reduce.4.cloned.1.call-done = f32[8,8192]{1,0:T(8,128)} async-done(((f32[8,8192]{1,0:T(8,128)}), f32[8,8192]{1,0:T(8,128)}) %all-reduce.4.cloned.1.call-update) | async-done | bytes 262160 | tf_op jit(solution)/shard_map/psum | solution.py:54
  181.2 24.6 %all_gather.20 = bf16[8,4096]{1,0:T(8,128)(2,1)S(1)} all-gather(bf16[8,128]{1,0:T(8,128)(2,1)S(1)} %subtract_convert_fusion.3), channel_id=1, replica_groups=mesh['leaf'=4,'rows'=32] {'rows'}, dimensions={1}, use_global_device_ids=true | all-gather | bytes 67584 | tf_op jit(solution)/shard_map/all_gather | solution.py:63
  206.2 21.5 %all_gather.21 = bf16[8,4096]{1,0:T(8,128)(2,1)S(1)} all-gather(bf16[8,128]{1,0:T(8,128)(2,1)S(1)} %get-tuple-element.24), channel_id=1, replica_groups=mesh['leaf'=4,'rows'=32] {'rows'}, dimensions={1}, use_global_device_ids=true | all-gather | bytes 67584 | tf_op jit(solution)/shard_map/all_gather | solution.py:69
  231.8 141.0 %all-reduce.8.cloned.1.call-done = f32[8,4096]{1,0:T(8,128)} async-done(((f32[8,4096]{1,0:T(8,128)}), f32[8,4096]{1,0:T(8,128)}) %all-reduce.8.cloned.1.call-update) | async-done | bytes 131088 | tf_op jit(solution)/shard_map/psum | solution.py:75
  372.8 41.1 %all-reduce.6.cloned.1.call-done = f32[8,4096]{1,0:T(8,128)} async-done(((f32[8,4096]{1,0:T(8,128)}), f32[8,4096]{1,0:T(8,128)}) %all-reduce.6.cloned.1.call-update) | async-done | bytes 131088 | tf_op jit(solution)/shard_map/psum | solution.py:56
  414.7 35.9 %all-gather = bf16[128,32,8]{1,2,0:T(8,128)(2,1)S(1)} all-gather(bf16[1,32,8]{1,2,0:T(8,128)(2,1)S(1)} %fusion.31), channel_id=1, replica_groups=mesh['leaf'=4,'rows'=32] {'leaf','rows'}, dimensions={0}, use_global_device_ids=true | all-gather | bytes 66048 | tf_op jit(solution)/shard_map/all_gather | solution.py:80
  455.2 5.4 collective-permute-done.1
  462.5 4.6 collective-permute-done.2
  467.6 4.6 collective-permute-done.3
  474.1 4.7 collective-permute-done.4
  483.3 70.2 %reduce-scatter.9.cloned.1.call-done = f32[8,128]{1,0:T(8,128)} async-done(((f32[8,4096]{1,0:T(8,128)}), f32[8,128]{1,0:T(8,128)}) %reduce-scatter.9.cloned.1.call-update) | async-done | bytes 4112 | tf_op jit(solution)/shard_map/reduce_scatter | solution.py:95
  555.7 73.1 %reduce-scatter.11.cloned.1.call-done = f32[8,128]{1,0:T(8,128)} async-done(((f32[8,4096]{1,0:T(8,128)}), f32[8,128]{1,0:T(8,128)}) %reduce-scatter.11.cloned.1.call-update) | async-done | bytes 4112 | tf_op jit(solution)/shard_map/reduce_scatter | solution.py:98
  629.5 23.6 %all_gather.23 = bf16[8,4096]{1,0:T(8,128)(2,1)S(1)} all-gather(bf16[8,128]{1,0:T(8,128)(2,1)S(1)} %convert_element_type.38), channel_id=1, replica_groups=mesh['leaf'=4,'rows'=32] {'rows'}, dimensions={1}, use_global_device_ids=true | all-gather | bytes 67584 | tf_op jit(solution)/shard_map/all_gather | solution.py:99
  654.1 3.7 gather_fusion.1
  663.8 4.5 reshape.143
  668.5 76.7 %reduce-scatter.13.cloned.1.call-done = f32[64,32]{1,0:T(8,128)} async-done(((f32[2048,32]{1,0:T(8,128)}), f32[64,32]{1,0:T(8,128)}) %reduce-scatter.13.cloned.1.call-update) | async-done | bytes 8208
  746.4 3.1 copy.78
  749.5 4.5 reshape.145
  754.7 76.7 %reduce-scatter.15.cloned.1.call-done = f32[64,32]{1,0:T(8,128)} async-done(((f32[2048,32]{1,0:T(8,128)}), f32[64,32]{1,0:T(8,128)}) %reduce-scatter.15.cloned.1.call-update) | async-done | bytes 8208
  (85 shorter events, 36.5 us)
Async XLA Ops:
  7.2 29.2 %copy-start = (bf16[4,64,2048]{2,1,0:T(8,128)(2,1)S(1)}, bf16[4,64,2048]{2,1,0:T(8,128)(2,1)}, u32[]{:S(2)}) copy-start(bf16[4,64,2048]{2,1,0:T(8,128)(2,1)} %param.15) | copy-start | bytes 3145732
  7.2 172.4 %all-reduce.4.cloned.1.call-start = ((), (), s32[]{:S(2)}) async-start(), calls=%async_computation.4 | async-start | bytes 524288 | tf_op jit(solution)/shard_map/psum | solution.py:54
  36.3 26.3 %copy-start.8 = (s32[4]{0:T(128)S(1)}, s32[4]{0:T(128)}, u32[]{:S(2)}) copy-start(s32[4]{0:T(128)} %param.18) | copy-start | bytes 52
  62.7 3.4 copy-start.5
  74.5 3.6 copy-start.9
  74.5 106.7 %copy-start.6 = (f32[8,1,128]{2,1,0:T(1,128)S(1)}, f32[8,1,128]{2,1,0:T(1,128)}, u32[]{:S(2)}) copy-start(f32[8,1,128]{2,1,0:T(1,128)} %param.13) | copy-start | bytes 12292
  74.5 131.4 %copy-start.3 = (bf16[1,128,4096]{2,1,0:T(8,128)(2,1)S(1)}, bf16[1,128,4096]{2,1,0:T(8,128)(2,1)}, u32[]{:S(2)}) copy-start(bf16[1,128,4096]{2,1,0:T(8,128)(2,1)} %param.19) | copy-start | bytes 3145732
  78.0 149.7 %copy-start.1 = (bf16[1,128,4096]{2,1,0:T(8,128)(2,1)S(1)}, bf16[1,128,4096]{2,1,0:T(8,128)(2,1)}, u32[]{:S(2)}) copy-start(bf16[1,128,4096]{2,1,0:T(8,128)(2,1)} %param.20) | copy-start | bytes 3145732
  78.1 294.7 %all-reduce.8.cloned.1.call-start = ((), (), s32[]{:S(2)}) async-start(), calls=%async_computation.6 | async-start | bytes 262144 | tf_op jit(solution)/shard_map/psum | solution.py:75
  228.2 185.7 %copy-start.7 = (f32[8,32]{1,0:T(8,128)S(1)}, f32[8,32]{1,0:T(8,128)}, u32[]{:S(2)}) copy-start(f32[8,32]{1,0:T(8,128)} %param.14) | copy-start | bytes 3076
  231.0 182.9 %all-reduce.6.cloned.1.call-start = ((), (), s32[]{:S(2)}) async-start(), calls=%async_computation.5 | async-start | bytes 262144 | tf_op jit(solution)/shard_map/psum | solution.py:56
  231.8 321.7 %reduce-scatter.9.cloned.1.call-start = ((), (), s32[]{:S(2)}) async-start(), calls=%async_computation.7 | async-start | bytes 135168 | tf_op jit(solution)/shard_map/reduce_scatter | solution.py:95
  453.3 28.8 %copy-start.2 = (bf16[1,128,4096]{2,1,0:T(8,128)(2,1)S(1)}, bf16[1,128,4096]{2,1,0:T(8,128)(2,1)}, u32[]{:S(2)}) copy-start(bf16[1,128,4096]{2,1,0:T(8,128)(2,1)} %param.20) | copy-start | bytes 3145732
  453.3 1.4 collective-permute-start
  454.7 98.7 %copy-start.4 = (bf16[1,128,4096]{2,1,0:T(8,128)(2,1)S(1)}, bf16[1,128,4096]{2,1,0:T(8,128)(2,1)}, u32[]{:S(2)}) copy-start(bf16[1,128,4096]{2,1,0:T(8,128)(2,1)} %param.19) | copy-start | bytes 3145732
  454.8 5.8 collective-permute-start.1
  460.6 6.6 collective-permute-start.2
  467.2 5.0 collective-permute-start.3
  472.3 6.6 collective-permute-start.4
  483.2 145.6 %reduce-scatter.11.cloned.1.call-start = ((), (), s32[]{:S(2)}) async-start(), calls=%async_computation.8 | async-start | bytes 135168 | tf_op jit(solution)/shard_map/reduce_scatter | solution.py:98
  555.1 190.1 %reduce-scatter.13.cloned.1.call-start = ((), (), s32[]{:S(2)}) async-start(), calls=%async_computation.9 | async-start | bytes 1081344
  668.4 163.0 %reduce-scatter.15.cloned.1.call-start = ((), (), s32[]{:S(2)}) async-start(), calls=%async_computation.10 | async-start | bytes 1081344
Sparse Core Ops, SparseCore 0:
  78.2 101.3 all-reduce.3
  231.2 141.6 all-reduce.7
  375.1 38.7 all-reduce.5
  483.3 70.0 reduce-scatter.8
  557.3 71.4 reduce-scatter.10
  668.5 76.6 reduce-scatter.12
  754.1 77.2 reduce-scatter.14
